TPU v7x, 32 devices: a whole 2x2x4 slice. The times are simulated.
32 devices in a mesh: gene: 4 (over x, core), site: 8 (over z, y).
Axes of the slice: x: 2, y: 2, z: 4, core: 2. Of those that a mesh axis runs over, the one named last changes fastest.
Arguments:
- tips: bfloat16 [4, 32, 20, 16384], P('gene', None, None, 'site'), may hold values from 0.0009994507 to 1
- exchange: float32 [20, 20], replicated, may hold values from 0.05 to 5
- freqs: float32 [20], replicated, may hold values from 0.02 to 0.12
- rates: float32 [4], replicated, may hold values from 0.1 to 3
- branch: float32 [62], replicated, may hold values from 0.02 to 0.6
- children: int32 [31, 2], replicated, may hold values from 0 to 61, as said below
- slot_gene: int32 [4, 128], P('gene', 'site'), may hold values from 0 to 63, as said below
- site_count: int32 [4, 128], P('gene', 'site'), may hold values from 0 to 128, as said below
Outputs:
- site_loglik: float32 [4, 16384], P('gene', 'site')
- gene_loglik: float32 [4, 64], P('gene')
- total: float32 [], replicated
Inputs may be any that keep to these rules, and one draw needn't show every extreme that they name: `children`: internal nodes come in 5 levels: the first 16 pair up all leaves, each next level pairs up all nodes of the level before, in node order; each node is a child once. On each device along site the slots with site_count > 0 come first; each device holds at least (64 + 8 - 1) // 8 of them and in each group one device has all 16 live; a live slot's live sites are its first ones. `slot_gene`: every gene of a group owns at least one live slot; on slots that are not live the value is 0.
All inputs are finite; a program needn't handle non-finite values.
Results may differ from a plain program's by a relative error of at most 0.0003.
Values may be sent and summed in bfloat16 or wider, within the bound.
No kernel may reach another device: no remote copies, remote signals or barrier semaphores. Data moves between devices by JAX's collectives and lax.ppermute only.
A program may use at most 128 MiB of HBM per device.

v0:
```python
import functools

import jax
import jax.numpy as jnp
from jax import lax
from jax.experimental import pallas as pl
from jax.experimental.pallas import tpu as pltpu
from jax.sharding import PartitionSpec as P

GROUP_GENES = 64
TAYLOR = 8
SQUARINGS = 8
LANES = 128
F32 = jnp.float32
BF16 = jnp.bfloat16


def up(value, to):
    return (value + to - 1) // to * to


def kernel(dims, *refs):
    taxa, states, cats, width, slots = dims
    levels = []
    count = taxa // 2
    while count > 1:
        levels.append(pltpu.VMEM((count, 3 * states * cats, width), BF16))
        count //= 2
    rows = states * cats
    half = up(states, 16)
    pl.run_scoped(
        functools.partial(body_of, dims, *refs),
        pltpu.VMEM((taxa, 2 * half, width), BF16),
        pltpu.VMEM((taxa, rows, LANES), BF16),
        pltpu.VMEM((taxa, rows, 2 * LANES), BF16),
        *levels,
    )


def body_of(
    dims,
    children,
    counts,
    genes,
    exchange,
    freqs,
    rates,
    branch,
    tips,
    site_out,
    part_out,
    raw,
    leaf_m,
    leaf_n,
    inner_m,
    inner_n,
    leaf_f,
    inner_f,
    scale,
    sem,
    leaves,
    leaf_p,
    inner_p,
    *levels,
):
    taxa, states, cats, width, slots = dims
    pad = up(states, 8)
    half = up(states, 16)
    rows = states * cats
    chunk = 256
    group = 8
    copy = pltpu.make_async_copy(tips.at[0], raw, sem)
    copy.start()

    row = lax.broadcasted_iota(jnp.int32, (states, states), 0)
    col = lax.broadcasted_iota(jnp.int32, (states, states), 1)
    eye = (row == col).astype(F32)
    sym = (exchange[...] + exchange[...].T) * 0.5 * (1.0 - eye)
    pi = freqs[...] / jnp.sum(freqs[...], axis=1, keepdims=True)
    root = jnp.sqrt(pi)
    root_t = jnp.sqrt(jnp.sum(eye * pi, axis=1, keepdims=True))
    qmat = sym * pi
    qmat = qmat - eye * jnp.sum(qmat, axis=1, keepdims=True)
    rate = -jnp.sum(jnp.sum(qmat * eye * pi, axis=1, keepdims=True), axis=0, keepdims=True)
    qmat = (sym * root * root_t + eye * qmat) / rate
    scaled = rates[...] / jnp.mean(rates[...], axis=1, keepdims=True)
    fill = jnp.zeros((1, 2 * taxa - branch.shape[1]), F32)
    lengths = jnp.concatenate([branch[...], fill], axis=1)
    times = [
        lengths[:, h * taxa : (h + 1) * taxa] * scaled[:, k : k + 1]
        for h in range(2)
        for k in range(cats)
    ]
    times = jnp.concatenate(times, axis=1) / 256.0
    batch = cats * taxa

    powers = [qmat]
    dot = functools.partial(jnp.dot, precision=lax.Precision.HIGHEST, preferred_element_type=F32)
    for order in range(2, TAYLOR + 1):
        lo = order // 2
        powers.append(dot(powers[lo - 1], powers[order - lo - 1]))
    fill = jnp.zeros((pad - states, states), F32)
    powers = [jnp.concatenate([p, fill], axis=0) for p in powers]
    times_b = jnp.broadcast_to(times, (pad, 2 * batch))
    for i in range(states):
        acc = jnp.zeros((pad, 2 * batch), F32)
        for order in range(TAYLOR, 0, -1):
            column = jnp.broadcast_to(powers[order - 1][:, i : i + 1], (pad, 2 * batch))
            acc = (column + acc) * (times_b * (1.0 / order))
        leaf_m[i] = acc[:, :batch]
        inner_m[i] = acc[:, batch:]

    def square(src, dst):
        def part(at, size, after=None):
            two = 2.0 if after is None else 2.0 + 0.0 * after[:1, :batch]
            low = at // 8 * 8
            acc = [src[at + q, low:, :] * two for q in range(size)]
            for j in range(states):
                right = src[j, low:, :]
                for q in range(size):
                    acc[q] = acc[q] + src[at + q, j : j + 1, :] * right
            for q in range(size):
                dst[at + q, low:, :] = acc[q]
                for tile in range(low + 8, pad, 8):
                    real = min(8, states - tile)
                    mirror = acc[q][tile - low : tile - low + real]
                    dst[tile : tile + real, at + q : at + q + 1, :] = mirror[:, None, :]

        pieces = []
        at = 0
        while at < states:
            size = min(2 << (at // 8), 8 - at % 8, states - at)
            pieces.append(functools.partial(part, at, size))
            at += size
        return pieces[::-1]

    target = lax.broadcasted_iota(jnp.int32, (group * half, group * states), 1)
    target = (target & (group - 1)) * half + (target >> 3)
    pick = lax.broadcasted_iota(jnp.int32, (group * half, group * states), 0) == target
    pick = pick.astype(F32).astype(BF16)
    chunks = width // chunk
    rounds = SQUARINGS // 2
    def leaf_step(step, carry):
        for src, dst in ((leaf_m, leaf_n), (leaf_n, leaf_m)):
            for piece in square(src, dst)[::-1]:
                piece()
        return carry

    lax.fori_loop(0, rounds, leaf_step, 0)

    def select(c, carry):
        cols = pl.ds(pl.multiple_of(c * chunk, chunk), chunk)
        for g in range(taxa // group):
            x = raw[:, pl.ds(g * group, group), cols].reshape(states * group, chunk)
            y = jnp.dot(pick, x, preferred_element_type=F32).astype(BF16)
            for one in range(group):
                z = y[one * half : (one + 1) * half]
                leaves[g * group + one, pl.ds(0, half), cols] = z
                leaves[g * group + one, pl.ds(half, half), cols] = z
        return carry

    copy.wait()
    lax.fori_loop(0, chunks, select, 0)

    sub = lax.broadcasted_iota(jnp.int32, (pad, batch), 0)
    root_w = jnp.concatenate([root_t, jnp.ones((pad - states, 1), F32)], axis=0)
    root_w = jnp.broadcast_to(root_w, (pad, batch))
    over = 1.0 / root_w
    across = lax.broadcasted_iota(jnp.int32, (taxa, LANES), 1)
    many = LANES // pad

    def spread(mat, to, turn):
        for start in range(0, states, many):
            size = min(many, states - start)
            tall = []
            for i in range(start, start + size):
                x = mat[i] * (root_w * over[i : i + 1]) + (sub == i).astype(F32)
                tall.append(x)
            tall.append(jnp.zeros((LANES - size * pad, batch), F32))
            z = jnp.concatenate(tall, axis=0).T
            for q in range(size):
                for k in range(cats):
                    at = k * states if turn else 0
                    part = z[k * taxa : (k + 1) * taxa]
                    shift = (at - q * pad) % LANES
                    if shift:
                        part = pltpu.roll(part, shift, 1)
                    part = jnp.where((across >= at) & (across < at + states), part, 0.0)
                    to[pl.ds((k * states + start + q) * (taxa + 1), taxa), :] = part

    spread(leaf_m, leaf_f, False)
    lane = lax.broadcasted_iota(jnp.int32, (rows, LANES), 1)

    unroll = 4

    def split_leaf(step, carry):
        for n in [step * unroll + u for u in range(unroll)]:
            x = leaf_f[pl.ds(n, rows, stride=taxa + 1), :]
            hi = x.astype(BF16).astype(F32)
            leaf_p[n] = (hi + pltpu.roll(x - hi, half, 1)).astype(BF16)
        return carry

    def split_inner(step, carry):
        for n in [step * unroll + u for u in range(unroll)]:
            x = inner_f[pl.ds(n, rows, stride=taxa + 1), :]
            hi = x.astype(BF16).astype(F32)
            turned = pltpu.roll(hi, rows, 1)
            low = pltpu.roll(x - hi, 2 * rows - LANES, 1)
            inner_p[n, :, pl.ds(0, LANES)] = jnp.where(lane < rows, hi, turned).astype(BF16)
            low = jnp.where(lane < 2 * rows - LANES, turned, low)
            inner_p[n, :, pl.ds(LANES, LANES)] = low.astype(BF16)
        return carry

    lax.fori_loop(0, taxa // unroll, split_leaf, 0)

    scale[...] = jnp.zeros_like(scale)

    def store(to, node, cols, p):
        hi = p.astype(BF16)
        lo = (p - hi.astype(F32)).astype(BF16)
        to[node, pl.ds(0, rows), cols] = hi
        to[node, pl.ds(rows, rows), cols] = lo
        to[node, pl.ds(2 * rows, rows), cols] = hi

    def messages(node, level, first):
        ids = [children[side, first + node] for side in range(2)]
        if level == 0:
            mats = [leaf_p[child, :, : 2 * half] for child in ids]
            source, base = leaves, 0
        else:
            mats = [inner_p[child - taxa, :, : 3 * rows] for child in ids]
            source, base = levels[level - 1], taxa + first - 2 * (taxa >> (level + 1))
        for c in range(chunks):
            cols = pl.ds(c * chunk, chunk)
            left, right = (
                jnp.dot(mat, source[child - base, :, cols], preferred_element_type=F32)
                for mat, child in zip(mats, ids)
            )
            yield c, cols, left * right

    def at_nodes(step, carry, level, first, each):
        parts, done = [], 0
        if level == 0:
            parts = square(inner_m, inner_n)
            parts = square(inner_n, inner_m) + parts
            total = len(parts)
            every = each * chunks / total
            parts.pop()()
        for u in range(each):
            node = step * each + u
            for c, cols, p in messages(node, level, first):
                if level % 3 == 2:
                    top = jnp.max(p, axis=0, keepdims=True)
                    p = p * (1.0 / top)
                    scale[:, cols] = scale[:, cols] + jnp.log(top)
                store(levels[level], node, cols, p)
                done += 1
                while parts and done >= every * (total - len(parts)):
                    parts.pop()(p)
        return carry

    first, count, level = 0, taxa // 2, 0
    assert count % rounds == 0
    while count > 1:
        each = 2 if level else count // rounds
        lax.fori_loop(
            0, count // each, functools.partial(at_nodes, level=level, first=first, each=each), 0
        )
        if level == 0:
            spread(inner_m, inner_f, True)
            lax.fori_loop(0, taxa // unroll, split_inner, 0)
        first, count, level = first + count, count // 2, level + 1

    wide = lax.broadcasted_iota(jnp.int32, (rows, states), 0)
    tall = lax.broadcasted_iota(jnp.int32, (rows, states), 1)
    weight = jnp.where(wide % states == tall, pi, 0.0)
    weight = jnp.sum(weight, axis=1, keepdims=True) / cats
    line = lax.broadcasted_iota(jnp.int32, (1, LANES), 1)
    tile = width // slots
    sums = jnp.zeros((1, LANES), F32)
    sizes = jnp.zeros((1, LANES), F32)
    whole = jnp.zeros((1, 1), F32)
    for c, cols, p in messages(0, level, first):
        lik = jnp.sum(p * weight, axis=0, keepdims=True)
        value = jnp.log(lik) + scale[:, cols]
        for t in range(chunk // tile):
            slot = c * (chunk // tile) + t
            size = counts[0, slot]
            part = jnp.where(line < size, value[:, t * tile : (t + 1) * tile], 0.0)
            site_out[:, pl.ds(slot * tile, tile)] = part
            sum_of = jnp.sum(part, axis=1, keepdims=True)
            hit = (line == genes[0, slot]) & (size > 0)
            sums = sums + jnp.where(hit, sum_of, 0.0)
            sizes = sizes + jnp.where(hit, size.astype(F32), 0.0)
            whole = whole + sum_of
    tail = jnp.where(line == 0, whole, 0.0)
    message_row = jnp.concatenate([sums, sizes, tail], axis=1)
    part_out[...] = jnp.broadcast_to(message_row[None], part_out.shape)


def on_device(tips, exchange, freqs, rates, branch, children, slot_gene, site_count):
    taxa, states, width = tips.shape[1:]
    slots = site_count.shape[1]
    cats = rates.shape[0]
    rows = states * cats
    members = lax.axis_size("site")
    groups = lax.axis_size("gene")
    devices = members * groups
    pad = up(states, 8)
    smem = pl.BlockSpec(memory_space=pltpu.SMEM)
    vmem = pl.BlockSpec(memory_space=pltpu.VMEM)
    levels = []
    count = taxa // 2
    while count > 1:
        levels.append(pltpu.VMEM((count, 3 * rows, width), BF16))
        count //= 2
    site, part = pl.pallas_call(
        functools.partial(kernel, (taxa, states, cats, width, slots)),
        out_shape=(
            jax.ShapeDtypeStruct((1, width), F32),
            jax.ShapeDtypeStruct((devices, 1, 3 * LANES), F32),
        ),
        in_specs=[smem] * 3 + [vmem] * 4 + [pl.BlockSpec(memory_space=pl.ANY)],
        out_specs=(vmem, vmem),
        scratch_shapes=[
            pltpu.VMEM((states, taxa, width), BF16),
            pltpu.VMEM((states, pad, cats * taxa), F32),
            pltpu.VMEM((states, pad, cats * taxa), F32),
            pltpu.VMEM((states, pad, cats * taxa), F32),
            pltpu.VMEM((states, pad, cats * taxa), F32),
            pltpu.VMEM(((taxa + 1) * rows, LANES), F32),
            pltpu.VMEM(((taxa + 1) * rows, LANES), F32),
            pltpu.VMEM((1, width), F32),
            pltpu.SemaphoreType.DMA,
        ],
        compiler_params=pltpu.CompilerParams(vmem_limit_bytes=60 * 1024 * 1024),
        name="prune",
    )(
        children.T,
        site_count,
        slot_gene,
        exchange,
        freqs[None],
        rates[None],
        branch[None],
        tips.transpose(0, 2, 1, 3),
    )
    table = lax.all_to_all(part, ("gene", "site"), split_axis=0, concat_axis=0, tiled=True)
    table = table.reshape(groups, members, 3 * LANES)
    mine = lax.dynamic_index_in_dim(table, lax.axis_index("gene"), 0, keepdims=False)
    mine = jnp.sum(mine, axis=0)
    gene = mine[:GROUP_GENES] / mine[LANES : LANES + GROUP_GENES]
    total = jnp.sum(table[:, :, 2 * LANES]) / (width * members)
    return site, gene[None, :], total


def solution(mesh):
    placed = (
        P("gene", None, None, "site"),
        P(),
        P(),
        P(),
        P(),
        P(),
        P("gene", "site"),
        P("gene", "site"),
    )
    return jax.shard_map(
        on_device,
        mesh=mesh,
        in_specs=placed,
        out_specs=(P("gene", "site"), P("gene", None), P()),
        check_vma=False,
    )
```

profile of v0, /device:TPU:0, one launch (start us, length us, event | category | flops | bytes accessed | tf_op | source)
XLA Modules:
  0.0 40.2 jit_solution(2279765739978675851)
XLA Ops:
  0.6 22.1 %prune.1 = (f32[1,2048]{1,0:T(1,128)}, f32[32,1,384]{2,1,0:T(1,128)}) custom-call(s32[2,31]{1,0:T(2,128)} %bitcast.13, s32[1,16]{1,0:T(1,128)} %refs_1_.1, s32[1,16]{1,0:T(1,128)} %refs_2_.1, f32[20,20]{1,0:T(8,128)} %refs_3_.1, f32[1,20]{1,0:T(1,128)} %bitcast.14, f32[1,4]{1,0:T(1,128)} %bitcast.15, f32[1,62]{1,0:T(1,128)} %bitcast.16, ...), custom_call_target="tpu_custom_call" | custom-call | tf_op jit(solution)/shard_map/prune/pallas_call | solution.py:317
  22.7 7.3 %all-to-all-start = ((f32[32,1,384]{2,1,0:T(1,128)}), f32[32,1,384]{2,1,0:T(1,128)S(1)}, u32[]{:S(2)}, u32[]{:S(2)}) async-start(f32[32,1,384]{2,1,0:T(1,128)} %get-tuple-element.6), calls=%async_computation | async-start | bytes 98304 | tf_op jit(solution)/shard_map/all_to_all | solution.py:348
  30.0 7.2 %all-to-all-done = f32[32,1,384]{2,1,0:T(1,128)S(1)} async-done(((f32[32,1,384]{2,1,0:T(1,128)}), f32[32,1,384]{2,1,0:T(1,128)S(1)}, u32[]{:S(2)}, u32[]{:S(2)}) %all-to-all-start) | async-done | bytes 49184 | tf_op jit(solution)/shard_map/all_to_all | solution.py:348
  37.3 0.6 %slice_reduce_fusion = f32[]{:T(128)} fusion(f32[4,8,384]{2,1,0:T(8,128)S(1)} %bitcast.11), kind=kLoop, calls=%fused_computation.1 | loop fusion | flops 31 | bytes 132 | tf_op jit(solution)/shard_map/reduce_sum | solution.py:353
  37.9 0.5 %fusion = f32[1,64]{1,0:T(1,128)} fusion(f32[384]{0:T(512)S(1)} %dynamic-slice_reduce_fusion), kind=kLoop, calls=%fused_computation.4 | loop fusion | flops 64 | bytes 768 | tf_op jit(solution)/shard_map/broadcast_in_dim | solution.py:354
  (2 shorter events, 0.0 us)
Async XLA Ops:
  22.7 14.6 %all-to-all-start = ((f32[32,1,384]{2,1,0:T(1,128)}), f32[32,1,384]{2,1,0:T(1,128)S(1)}, u32[]{:S(2)}, u32[]{:S(2)}) async-start(f32[32,1,384]{2,1,0:T(1,128)} %get-tuple-element.6), calls=%async_computation | async-start | bytes 98304 | tf_op jit(solution)/shard_map/all_to_all | solution.py:348
where the time goes:
time: 40.4 us; the launch traced here: 40.2 us
  Pallas kernels  22.1 us (55%)
  starting transfers between devices  7.33 us (18%)
  waiting for transfers between devices  7.23 us (18%)
  between operations  2.43 us (6%)
  other arithmetic  1.15 us (3%)
    pallas_call x1, Pallas kernels, on_device(): pl.pallas_call(functools.partial(kernel, (taxa, states, cats, width, slot...  22.1 us
    all_to_all x1, starting transfers between devices, on_device(): lax.all_to_all(part, ('gene', 'site'), split_axis=0, concat_axis=0, tiled...  7.33 us
    all_to_all x1, waiting for transfers between devices, on_device(): lax.all_to_all(part, ('gene', 'site'), split_axis=0, concat_axis=0, tiled...  7.23 us
  transfers between devices with their start and end apart: 1, of which 1 were waited for; matrix products, arithmetic and copies ran while one was open for 0% of the time, Pallas kernels for 0%

commit v1 on v0

--- a/solution.py
+++ b/solution.py
@@ -24,7 +24,7 @@
     levels = []
     count = taxa // 2
     while count > 1:
-        levels.append(pltpu.VMEM((count, 3 * states * cats, width), BF16))
+        levels.append(pltpu.VMEM((count, 2 * states * cats, width), BF16))
         count //= 2
     rows = states * cats
     half = up(states, 16)
@@ -32,7 +32,7 @@
         functools.partial(body_of, dims, *refs),
         pltpu.VMEM((taxa, 2 * half, width), BF16),
         pltpu.VMEM((taxa, rows, LANES), BF16),
-        pltpu.VMEM((taxa, rows, 2 * LANES), BF16),
+        pltpu.VMEM((taxa, 2 * rows, 2 * LANES), BF16),
         *levels,
     )
 
@@ -111,10 +111,9 @@
         inner_m[i] = acc[:, batch:]
 
     def square(src, dst):
-        def part(at, size, after=None):
-            two = 2.0 if after is None else 2.0 + 0.0 * after[:1, :batch]
+        def part(at, size):
             low = at // 8 * 8
-            acc = [src[at + q, low:, :] * two for q in range(size)]
+            acc = [src[at + q, low:, :] * 2.0 for q in range(size)]
             for j in range(states):
                 right = src[j, low:, :]
                 for q in range(size):
@@ -129,7 +128,7 @@
         pieces = []
         at = 0
         while at < states:
-            size = min(2 << (at // 8), 8 - at % 8, states - at)
+            size = min(4 << (at // 8), 8 - at % 8, states - at)
             pieces.append(functools.partial(part, at, size))
             at += size
         return pieces[::-1]
@@ -140,27 +139,38 @@
     pick = pick.astype(F32).astype(BF16)
     chunks = width // chunk
     rounds = SQUARINGS // 2
-    def leaf_step(step, carry):
-        for src, dst in ((leaf_m, leaf_n), (leaf_n, leaf_m)):
-            for piece in square(src, dst)[::-1]:
-                piece()
+    groups = taxa // group
+
+    def select(c, g):
+        cols = pl.ds(pl.multiple_of(c * chunk, chunk), chunk)
+        x = raw[:, pl.ds(g * group, group), cols].reshape(states * group, chunk)
+        y = jnp.dot(pick, x, preferred_element_type=F32)
+        z = y.astype(BF16)
+        for one in range(group):
+            part = z[one * half : (one + 1) * half]
+            leaves[g * group + one, pl.ds(0, half), cols] = part
+            leaves[g * group + one, pl.ds(half, half), cols] = part
+
+    def leaf_step(step, carry, beside):
+        parts = square(leaf_n, leaf_m) + square(leaf_m, leaf_n)
+        total = len(parts)
+        work = [(c, g) for c in range(beside) for g in range(groups)]
+        if not work:
+            while parts:
+                parts.pop()()
+        else:
+            parts.pop()()
+        for done, (c, g) in enumerate(work):
+            select(step * beside + c, g)
+            while parts and (done + 1) * total >= len(work) * (total - len(parts)):
+                parts.pop()()
         return carry
 
-    lax.fori_loop(0, rounds, leaf_step, 0)
-
-    def select(c, carry):
-        cols = pl.ds(pl.multiple_of(c * chunk, chunk), chunk)
-        for g in range(taxa // group):
-            x = raw[:, pl.ds(g * group, group), cols].reshape(states * group, chunk)
-            y = jnp.dot(pick, x, preferred_element_type=F32).astype(BF16)
-            for one in range(group):
-                z = y[one * half : (one + 1) * half]
-                leaves[g * group + one, pl.ds(0, half), cols] = z
-                leaves[g * group + one, pl.ds(half, half), cols] = z
-        return carry
-
+    early = rounds // 2
+    lax.fori_loop(0, early, functools.partial(leaf_step, beside=0), 0)
     copy.wait()
-    lax.fori_loop(0, chunks, select, 0)
+    late = rounds - early
+    lax.fori_loop(0, late, functools.partial(leaf_step, beside=chunks // late), 0)
 
     sub = lax.broadcasted_iota(jnp.int32, (pad, batch), 0)
     root_w = jnp.concatenate([root_t, jnp.ones((pad - states, 1), F32)], axis=0)
@@ -205,10 +215,10 @@
             x = inner_f[pl.ds(n, rows, stride=taxa + 1), :]
             hi = x.astype(BF16).astype(F32)
             turned = pltpu.roll(hi, rows, 1)
-            low = pltpu.roll(x - hi, 2 * rows - LANES, 1)
-            inner_p[n, :, pl.ds(0, LANES)] = jnp.where(lane < rows, hi, turned).astype(BF16)
-            low = jnp.where(lane < 2 * rows - LANES, turned, low)
-            inner_p[n, :, pl.ds(LANES, LANES)] = low.astype(BF16)
+            inner_p[n, :rows, :LANES] = jnp.where(lane < rows, hi, turned).astype(BF16)
+            inner_p[n, :rows, LANES:] = jnp.where(lane < 2 * rows - LANES, turned, 0.0).astype(BF16)
+            inner_p[n, rows:, :LANES] = (x - hi).astype(BF16)
+            inner_p[n, rows:, LANES:] = jnp.zeros((rows, LANES), BF16)
         return carry
 
     lax.fori_loop(0, taxa // unroll, split_leaf, 0)
@@ -220,7 +230,6 @@
         lo = (p - hi.astype(F32)).astype(BF16)
         to[node, pl.ds(0, rows), cols] = hi
         to[node, pl.ds(rows, rows), cols] = lo
-        to[node, pl.ds(2 * rows, rows), cols] = hi
 
     def messages(node, level, first):
         ids = [children[side, first + node] for side in range(2)]
@@ -228,7 +237,7 @@
             mats = [leaf_p[child, :, : 2 * half] for child in ids]
             source, base = leaves, 0
         else:
-            mats = [inner_p[child - taxa, :, : 3 * rows] for child in ids]
+            mats = [inner_p[child - taxa, :, : 2 * rows] for child in ids]
             source, base = levels[level - 1], taxa + first - 2 * (taxa >> (level + 1))
         for c in range(chunks):
             cols = pl.ds(c * chunk, chunk)
@@ -236,6 +245,8 @@
                 jnp.dot(mat, source[child - base, :, cols], preferred_element_type=F32)
                 for mat, child in zip(mats, ids)
             )
+            if level:
+                left, right = (side[:rows] + side[rows:] for side in (left, right))
             yield c, cols, left * right
 
     def at_nodes(step, carry, level, first, each):
@@ -256,7 +267,7 @@
                 store(levels[level], node, cols, p)
                 done += 1
                 while parts and done >= every * (total - len(parts)):
-                    parts.pop()(p)
+                    parts.pop()()
         return carry
 
     first, count, level = 0, taxa // 2, 0

time: 40.4 us -> 38.7 us (0.958)
  Pallas kernels: 22.1 us -> 20.4 us
    pallas_call x1, Pallas kernels: 22.1 us -> 20.4 us  [on_device(): pl.pallas_call(functools.partial(kernel, (taxa, states, cats, width, slot...]
where the time goes in v1:
time: 38.7 us; the launch traced here: 38.5 us
  Pallas kernels  20.4 us (53%)
  starting transfers between devices  7.34 us (19%)
  waiting for transfers between devices  7.23 us (19%)
  between operations  2.43 us (6%)
  other arithmetic  1.15 us (3%)
    pallas_call x1, Pallas kernels, on_device(): pl.pallas_call(functools.partial(kernel, (taxa, states, cats, width, slot...  20.4 us
    all_to_all x1, starting transfers between devices, on_device(): lax.all_to_all(part, ('gene', 'site'), split_axis=0, concat_axis=0, tiled...  7.34 us
    all_to_all x1, waiting for transfers between devices, on_device(): lax.all_to_all(part, ('gene', 'site'), split_axis=0, concat_axis=0, tiled...  7.23 us
  transfers between devices with their start and end apart: 1, of which 1 were waited for; matrix products, arithmetic and copies ran while one was open for 0% of the time, Pallas kernels for 0%

profile of v1, /device:TPU:0, one launch (start us, length us, event | category | flops | bytes accessed | tf_op | source)
XLA Modules:
  0.0 38.5 jit_solution(5814069405348056596)
XLA Ops:
  0.6 20.4 %prune.1 = (f32[1,2048]{1,0:T(1,128)}, f32[32,1,384]{2,1,0:T(1,128)}) custom-call(s32[2,31]{1,0:T(2,128)} %bitcast.13, s32[1,16]{1,0:T(1,128)} %refs_1_.1, s32[1,16]{1,0:T(1,128)} %refs_2_.1, f32[20,20]{1,0:T(8,128)} %refs_3_.1, f32[1,20]{1,0:T(1,128)} %bitcast.14, f32[1,4]{1,0:T(1,128)} %bitcast.15, f32[1,62]{1,0:T(1,128)} %bitcast.16, ...), custom_call_target="tpu_custom_call" | custom-call | tf_op jit(solution)/shard_map/prune/pallas_call | solution.py:328
  21.0 7.3 %all-to-all-start = ((f32[32,1,384]{2,1,0:T(1,128)}), f32[32,1,384]{2,1,0:T(1,128)S(1)}, u32[]{:S(2)}, u32[]{:S(2)}) async-start(f32[32,1,384]{2,1,0:T(1,128)} %get-tuple-element.6), calls=%async_computation | async-start | bytes 98304 | tf_op jit(solution)/shard_map/all_to_all | solution.py:359
  28.4 7.2 %all-to-all-done = f32[32,1,384]{2,1,0:T(1,128)S(1)} async-done(((f32[32,1,384]{2,1,0:T(1,128)}), f32[32,1,384]{2,1,0:T(1,128)S(1)}, u32[]{:S(2)}, u32[]{:S(2)}) %all-to-all-start) | async-done | bytes 49184 | tf_op jit(solution)/shard_map/all_to_all | solution.py:359
  35.6 0.6 %slice_reduce_fusion = f32[]{:T(128)} fusion(f32[4,8,384]{2,1,0:T(8,128)S(1)} %bitcast.11), kind=kLoop, calls=%fused_computation.1 | loop fusion | flops 31 | bytes 132 | tf_op jit(solution)/shard_map/reduce_sum | solution.py:364
  36.2 0.5 %fusion = f32[1,64]{1,0:T(1,128)} fusion(f32[384]{0:T(512)S(1)} %dynamic-slice_reduce_fusion), kind=kLoop, calls=%fused_computation.4 | loop fusion | flops 64 | bytes 768 | tf_op jit(solution)/shard_map/broadcast_in_dim | solution.py:365
  (2 shorter events, 0.0 us)
Async XLA Ops:
  21.0 14.6 %all-to-all-start = ((f32[32,1,384]{2,1,0:T(1,128)}), f32[32,1,384]{2,1,0:T(1,128)S(1)}, u32[]{:S(2)}, u32[]{:S(2)}) async-start(f32[32,1,384]{2,1,0:T(1,128)} %get-tuple-element.6), calls=%async_computation | async-start | bytes 98304 | tf_op jit(solution)/shard_map/all_to_all | solution.py:359

commit v2 on v1

--- a/solution.py
+++ b/solution.py
@@ -32,6 +32,7 @@
         functools.partial(body_of, dims, *refs),
         pltpu.VMEM((taxa, 2 * half, width), BF16),
         pltpu.VMEM((taxa, rows, LANES), BF16),
+        pltpu.VMEM((8 * half, 8 * states), BF16),
         pltpu.VMEM((taxa, 2 * rows, 2 * LANES), BF16),
         *levels,
     )
@@ -60,6 +61,7 @@
     sem,
     leaves,
     leaf_p,
+    picks,
     inner_p,
     *levels,
 ):
@@ -101,16 +103,24 @@
         powers.append(dot(powers[lo - 1], powers[order - lo - 1]))
     fill = jnp.zeros((pad - states, states), F32)
     powers = [jnp.concatenate([p, fill], axis=0) for p in powers]
-    times_b = jnp.broadcast_to(times, (pad, 2 * batch))
+    def put(dst, i, low, value):
+        dst[i, low:, :] = value
+        for tile in range(low + 8, pad, 8):
+            real = min(8, states - tile)
+            mirror = value[tile - low : tile - low + real]
+            dst[tile : tile + real, i : i + 1, :] = mirror[:, None, :]
+
     for i in range(states):
-        acc = jnp.zeros((pad, 2 * batch), F32)
+        low = i // 8 * 8
+        times_b = jnp.broadcast_to(times, (pad - low, 2 * batch))
+        acc = jnp.zeros((pad - low, 2 * batch), F32)
         for order in range(TAYLOR, 0, -1):
-            column = jnp.broadcast_to(powers[order - 1][:, i : i + 1], (pad, 2 * batch))
+            column = jnp.broadcast_to(powers[order - 1][low:, i : i + 1], acc.shape)
             acc = (column + acc) * (times_b * (1.0 / order))
-        leaf_m[i] = acc[:, :batch]
-        inner_m[i] = acc[:, batch:]
-
-    def square(src, dst):
+        put(leaf_m, i, low, acc[:, :batch])
+        put(inner_m, i, low, acc[:, batch:])
+
+    def square(src, dst, most):
         def part(at, size):
             low = at // 8 * 8
             acc = [src[at + q, low:, :] * 2.0 for q in range(size)]
@@ -119,16 +129,12 @@
                 for q in range(size):
                     acc[q] = acc[q] + src[at + q, j : j + 1, :] * right
             for q in range(size):
-                dst[at + q, low:, :] = acc[q]
-                for tile in range(low + 8, pad, 8):
-                    real = min(8, states - tile)
-                    mirror = acc[q][tile - low : tile - low + real]
-                    dst[tile : tile + real, at + q : at + q + 1, :] = mirror[:, None, :]
+                put(dst, at + q, low, acc[q])
 
         pieces = []
         at = 0
         while at < states:
-            size = min(4 << (at // 8), 8 - at % 8, states - at)
+            size = min(most, 8 - at % 8, states - at)
             pieces.append(functools.partial(part, at, size))
             at += size
         return pieces[::-1]
@@ -136,7 +142,7 @@
     target = lax.broadcasted_iota(jnp.int32, (group * half, group * states), 1)
     target = (target & (group - 1)) * half + (target >> 3)
     pick = lax.broadcasted_iota(jnp.int32, (group * half, group * states), 0) == target
-    pick = pick.astype(F32).astype(BF16)
+    picks[...] = pick.astype(F32).astype(BF16)
     chunks = width // chunk
     rounds = SQUARINGS // 2
     groups = taxa // group
@@ -144,7 +150,7 @@
     def select(c, g):
         cols = pl.ds(pl.multiple_of(c * chunk, chunk), chunk)
         x = raw[:, pl.ds(g * group, group), cols].reshape(states * group, chunk)
-        y = jnp.dot(pick, x, preferred_element_type=F32)
+        y = jnp.dot(picks[...], x, preferred_element_type=F32)
         z = y.astype(BF16)
         for one in range(group):
             part = z[one * half : (one + 1) * half]
@@ -152,7 +158,7 @@
             leaves[g * group + one, pl.ds(half, half), cols] = part
 
     def leaf_step(step, carry, beside):
-        parts = square(leaf_n, leaf_m) + square(leaf_m, leaf_n)
+        parts = square(leaf_n, leaf_m, 8) + square(leaf_m, leaf_n, 8)
         total = len(parts)
         work = [(c, g) for c in range(beside) for g in range(groups)]
         if not work:
@@ -252,8 +258,8 @@
     def at_nodes(step, carry, level, first, each):
         parts, done = [], 0
         if level == 0:
-            parts = square(inner_m, inner_n)
-            parts = square(inner_n, inner_m) + parts
+            parts = square(inner_m, inner_n, 8)
+            parts = square(inner_n, inner_m, 2) + parts
             total = len(parts)
             every = each * chunks / total
             parts.pop()()
@@ -273,7 +279,7 @@
     first, count, level = 0, taxa // 2, 0
     assert count % rounds == 0
     while count > 1:
-        each = 2 if level else count // rounds
+        each = min(4, count) if level else count // rounds
         lax.fori_loop(
             0, count // each, functools.partial(at_nodes, level=level, first=first, each=each), 0
         )
@@ -289,8 +295,6 @@
     line = lax.broadcasted_iota(jnp.int32, (1, LANES), 1)
     tile = width // slots
     sums = jnp.zeros((1, LANES), F32)
-    sizes = jnp.zeros((1, LANES), F32)
-    whole = jnp.zeros((1, 1), F32)
     for c, cols, p in messages(0, level, first):
         lik = jnp.sum(p * weight, axis=0, keepdims=True)
         value = jnp.log(lik) + scale[:, cols]
@@ -300,13 +304,10 @@
             part = jnp.where(line < size, value[:, t * tile : (t + 1) * tile], 0.0)
             site_out[:, pl.ds(slot * tile, tile)] = part
             sum_of = jnp.sum(part, axis=1, keepdims=True)
-            hit = (line == genes[0, slot]) & (size > 0)
-            sums = sums + jnp.where(hit, sum_of, 0.0)
-            sizes = sizes + jnp.where(hit, size.astype(F32), 0.0)
-            whole = whole + sum_of
-    tail = jnp.where(line == 0, whole, 0.0)
-    message_row = jnp.concatenate([sums, sizes, tail], axis=1)
-    part_out[...] = jnp.broadcast_to(message_row[None], part_out.shape)
+            gene = jnp.where(size > 0, genes[0, slot], 2 * GROUP_GENES)
+            sums = sums + jnp.where(line == gene, sum_of, 0.0)
+            sums = sums + jnp.where(line == gene + GROUP_GENES, size.astype(F32), 0.0)
+    part_out[...] = jnp.broadcast_to(sums[None], part_out.shape)
 
 
 def on_device(tips, exchange, freqs, rates, branch, children, slot_gene, site_count):
@@ -329,7 +330,7 @@
         functools.partial(kernel, (taxa, states, cats, width, slots)),
         out_shape=(
             jax.ShapeDtypeStruct((1, width), F32),
-            jax.ShapeDtypeStruct((devices, 1, 3 * LANES), F32),
+            jax.ShapeDtypeStruct((devices, 1, 2 * GROUP_GENES), F32),
         ),
         in_specs=[smem] * 3 + [vmem] * 4 + [pl.BlockSpec(memory_space=pl.ANY)],
         out_specs=(vmem, vmem),
@@ -357,11 +358,11 @@
         tips.transpose(0, 2, 1, 3),
     )
     table = lax.all_to_all(part, ("gene", "site"), split_axis=0, concat_axis=0, tiled=True)
-    table = table.reshape(groups, members, 3 * LANES)
+    table = table.reshape(groups, members, 2 * GROUP_GENES)
     mine = lax.dynamic_index_in_dim(table, lax.axis_index("gene"), 0, keepdims=False)
     mine = jnp.sum(mine, axis=0)
-    gene = mine[:GROUP_GENES] / mine[LANES : LANES + GROUP_GENES]
-    total = jnp.sum(table[:, :, 2 * LANES]) / (width * members)
+    gene = mine[:GROUP_GENES] / mine[GROUP_GENES:]
+    total = jnp.sum(table[:, :, :GROUP_GENES]) / (width * members)
     return site, gene[None, :], total
 
 

time: 38.7 us -> 37.9 us (0.979)
  Pallas kernels: 20.4 us -> 19.6 us
    pallas_call x1, Pallas kernels: 20.4 us -> 19.6 us  [on_device(): pl.pallas_call(functools.partial(kernel, (taxa, states, cats, width, slot...]
where the time goes in v2:
time: 37.9 us; the launch traced here: 37.7 us
  Pallas kernels  19.6 us (52%)
  starting transfers between devices  7.34 us (19%)
  waiting for transfers between devices  7.14 us (19%)
  between operations  2.43 us (6%)
  other arithmetic  1.21 us (3%)
    pallas_call x1, Pallas kernels, on_device(): pl.pallas_call(functools.partial(kernel, (taxa, states, cats, width, slot...  19.6 us
    all_to_all x1, starting transfers between devices, on_device(): lax.all_to_all(part, ('gene', 'site'), split_axis=0, concat_axis=0, tiled...  7.34 us
    all_to_all x1, waiting for transfers between devices, on_device(): lax.all_to_all(part, ('gene', 'site'), split_axis=0, concat_axis=0, tiled...  7.14 us
  transfers between devices with their start and end apart: 1, of which 1 were waited for; matrix products, arithmetic and copies ran while one was open for 0% of the time, Pallas kernels for 0%

profile of v2, /device:TPU:0, one launch (start us, length us, event | category | flops | bytes accessed | tf_op | source)
XLA Modules:
  0.0 37.7 jit_solution(92916184331782046)
XLA Ops:
  0.6 19.6 %prune.1 = (f32[1,2048]{1,0:T(1,128)}, f32[32,1,128]{2,1,0:T(1,128)}) custom-call(s32[2,31]{1,0:T(2,128)} %bitcast.11, s32[1,16]{1,0:T(1,128)} %refs_1_.1, s32[1,16]{1,0:T(1,128)} %refs_2_.1, f32[20,20]{1,0:T(8,128)} %refs_3_.1, f32[1,20]{1,0:T(1,128)} %bitcast.12, f32[1,4]{1,0:T(1,128)} %bitcast.13, f32[1,62]{1,0:T(1,128)} %bitcast.14, ...), custom_call_target="tpu_custom_call" | custom-call | tf_op jit(solution)/shard_map/prune/pallas_call | solution.py:329
  20.2 7.3 %all-to-all-start = ((f32[32,1,128]{2,1,0:T(1,128)}), f32[32,1,128]{2,1,0:T(1,128)S(1)}, u32[]{:S(2)}, u32[]{:S(2)}) async-start(f32[32,1,128]{2,1,0:T(1,128)} %get-tuple-element.6), calls=%async_computation | async-start | bytes 32768 | tf_op jit(solution)/shard_map/all_to_all | solution.py:360
  27.6 7.1 %all-to-all-done = f32[32,1,128]{2,1,0:T(1,128)S(1)} async-done(((f32[32,1,128]{2,1,0:T(1,128)}), f32[32,1,128]{2,1,0:T(1,128)S(1)}, u32[]{:S(2)}, u32[]{:S(2)}) %all-to-all-start) | async-done | bytes 16416 | tf_op jit(solution)/shard_map/all_to_all | solution.py:360
  34.7 0.6 %slice_reduce_fusion = f32[]{:T(128)} fusion(f32[4,8,128]{2,1,0:T(8,128)S(1)} %bitcast.9), kind=kLoop, calls=%fused_computation | loop fusion | flops 2047 | bytes 8196 | tf_op jit(solution)/shard_map/reduce_sum | solution.py:365
  35.3 0.6 %fusion = f32[1,64]{1,0:T(1,128)} fusion(f32[128]{0:T(128)S(1)} %dynamic-slice_reduce_fusion), kind=kLoop, calls=%fused_computation.3 | loop fusion | flops 64 | bytes 768 | tf_op jit(solution)/shard_map/broadcast_in_dim | solution.py:366
  (1 shorter events, 0.0 us)
Async XLA Ops:
  20.2 14.5 %all-to-all-start = ((f32[32,1,128]{2,1,0:T(1,128)}), f32[32,1,128]{2,1,0:T(1,128)S(1)}, u32[]{:S(2)}, u32[]{:S(2)}) async-start(f32[32,1,128]{2,1,0:T(1,128)} %get-tuple-element.6), calls=%async_computation | async-start | bytes 32768 | tf_op jit(solution)/shard_map/all_to_all | solution.py:360

commit v3 on v2

--- a/solution.py
+++ b/solution.py
@@ -207,7 +207,7 @@
     spread(leaf_m, leaf_f, False)
     lane = lax.broadcasted_iota(jnp.int32, (rows, LANES), 1)
 
-    unroll = 4
+    unroll = 8
 
     def split_leaf(step, carry):
         for n in [step * unroll + u for u in range(unroll)]:
@@ -340,8 +340,8 @@
             pltpu.VMEM((states, pad, cats * taxa), F32),
             pltpu.VMEM((states, pad, cats * taxa), F32),
             pltpu.VMEM((states, pad, cats * taxa), F32),
-            pltpu.VMEM(((taxa + 1) * rows, LANES), F32),
-            pltpu.VMEM(((taxa + 1) * rows, LANES), F32),
+            pltpu.VMEM(((taxa + 1) * (rows + 8), LANES), F32),
+            pltpu.VMEM(((taxa + 1) * (rows + 8), LANES), F32),
             pltpu.VMEM((1, width), F32),
             pltpu.SemaphoreType.DMA,
         ],

time: 37.9 us -> 37.5 us (0.989)
  Pallas kernels: 19.6 us -> 19.2 us
    pallas_call x1, Pallas kernels: 19.6 us -> 19.2 us  [on_device(): pl.pallas_call(functools.partial(kernel, (taxa, states, cats, width, slot...]
where the time goes in v3:
time: 37.5 us; the launch traced here: 37.3 us
  Pallas kernels  19.2 us (51%)
  starting transfers between devices  7.34 us (20%)
  waiting for transfers between devices  7.14 us (19%)
  between operations  2.43 us (6%)
  other arithmetic  1.21 us (3%)
    pallas_call x1, Pallas kernels, on_device(): pl.pallas_call(functools.partial(kernel, (taxa, states, cats, width, slot...  19.2 us
    all_to_all x1, starting transfers between devices, on_device(): lax.all_to_all(part, ('gene', 'site'), split_axis=0, concat_axis=0, tiled...  7.34 us
    all_to_all x1, waiting for transfers between devices, on_device(): lax.all_to_all(part, ('gene', 'site'), split_axis=0, concat_axis=0, tiled...  7.14 us
  transfers between devices with their start and end apart: 1, of which 1 were waited for; matrix products, arithmetic and copies ran while one was open for 0% of the time, Pallas kernels for 0%

profile of v3, /device:TPU:0, one launch (start us, length us, event | category | flops | bytes accessed | tf_op | source)
XLA Modules:
  0.0 37.3 jit_solution(1619534169968535435)
XLA Ops:
  0.6 19.2 %prune.1 = (f32[1,2048]{1,0:T(1,128)}, f32[32,1,128]{2,1,0:T(1,128)}) custom-call(s32[2,31]{1,0:T(2,128)} %bitcast.11, s32[1,16]{1,0:T(1,128)} %refs_1_.1, s32[1,16]{1,0:T(1,128)} %refs_2_.1, f32[20,20]{1,0:T(8,128)} %refs_3_.1, f32[1,20]{1,0:T(1,128)} %bitcast.12, f32[1,4]{1,0:T(1,128)} %bitcast.13, f32[1,62]{1,0:T(1,128)} %bitcast.14, ...), custom_call_target="tpu_custom_call" | custom-call | tf_op jit(solution)/shard_map/prune/pallas_call | solution.py:329
  19.8 7.3 %all-to-all-start = ((f32[32,1,128]{2,1,0:T(1,128)}), f32[32,1,128]{2,1,0:T(1,128)S(1)}, u32[]{:S(2)}, u32[]{:S(2)}) async-start(f32[32,1,128]{2,1,0:T(1,128)} %get-tuple-element.6), calls=%async_computation | async-start | bytes 32768 | tf_op jit(solution)/shard_map/all_to_all | solution.py:360
  27.2 7.1 %all-to-all-done = f32[32,1,128]{2,1,0:T(1,128)S(1)} async-done(((f32[32,1,128]{2,1,0:T(1,128)}), f32[32,1,128]{2,1,0:T(1,128)S(1)}, u32[]{:S(2)}, u32[]{:S(2)}) %all-to-all-start) | async-done | bytes 16416 | tf_op jit(solution)/shard_map/all_to_all | solution.py:360
  34.3 0.6 %slice_reduce_fusion = f32[]{:T(128)} fusion(f32[4,8,128]{2,1,0:T(8,128)S(1)} %bitcast.9), kind=kLoop, calls=%fused_computation | loop fusion | flops 2047 | bytes 8196 | tf_op jit(solution)/shard_map/reduce_sum | solution.py:365
  34.9 0.6 %fusion = f32[1,64]{1,0:T(1,128)} fusion(f32[128]{0:T(128)S(1)} %dynamic-slice_reduce_fusion), kind=kLoop, calls=%fused_computation.3 | loop fusion | flops 64 | bytes 768 | tf_op jit(solution)/shard_map/broadcast_in_dim | solution.py:366
  (1 shorter events, 0.0 us)
Async XLA Ops:
  19.8 14.5 %all-to-all-start = ((f32[32,1,128]{2,1,0:T(1,128)}), f32[32,1,128]{2,1,0:T(1,128)S(1)}, u32[]{:S(2)}, u32[]{:S(2)}) async-start(f32[32,1,128]{2,1,0:T(1,128)} %get-tuple-element.6), calls=%async_computation | async-start | bytes 32768 | tf_op jit(solution)/shard_map/all_to_all | solution.py:360

commit v4 on v3

--- a/solution.py
+++ b/solution.py
@@ -207,7 +207,7 @@
     spread(leaf_m, leaf_f, False)
     lane = lax.broadcasted_iota(jnp.int32, (rows, LANES), 1)
 
-    unroll = 8
+    unroll = 16
 
     def split_leaf(step, carry):
         for n in [step * unroll + u for u in range(unroll)]:

time: 37.5 us -> 37.2 us (level)
  no operation moved by 1% of the time
where the time goes in v4:
time: 37.2 us; the launch traced here: 37 us
  Pallas kernels  18.9 us (51%)
  starting transfers between devices  7.33 us (20%)
  waiting for transfers between devices  7.14 us (19%)
  between operations  2.43 us (7%)
  other arithmetic  1.21 us (3%)
    pallas_call x1, Pallas kernels, on_device(): pl.pallas_call(functools.partial(kernel, (taxa, states, cats, width, slot...  18.9 us
    all_to_all x1, starting transfers between devices, on_device(): lax.all_to_all(part, ('gene', 'site'), split_axis=0, concat_axis=0, tiled...  7.33 us
    all_to_all x1, waiting for transfers between devices, on_device(): lax.all_to_all(part, ('gene', 'site'), split_axis=0, concat_axis=0, tiled...  7.14 us
  transfers between devices with their start and end apart: 1, of which 1 were waited for; matrix products, arithmetic and copies ran while one was open for 0% of the time, Pallas kernels for 0%

profile of v4, /device:TPU:0, one launch (start us, length us, event | category | flops | bytes accessed | tf_op | source)
XLA Modules:
  0.0 37.0 jit_solution(22519202509021865)
XLA Ops:
  0.6 18.9 %prune.1 = (f32[1,2048]{1,0:T(1,128)}, f32[32,1,128]{2,1,0:T(1,128)}) custom-call(s32[2,31]{1,0:T(2,128)} %bitcast.11, s32[1,16]{1,0:T(1,128)} %refs_1_.1, s32[1,16]{1,0:T(1,128)} %refs_2_.1, f32[20,20]{1,0:T(8,128)} %refs_3_.1, f32[1,20]{1,0:T(1,128)} %bitcast.12, f32[1,4]{1,0:T(1,128)} %bitcast.13, f32[1,62]{1,0:T(1,128)} %bitcast.14, ...), custom_call_target="tpu_custom_call" | custom-call | tf_op jit(solution)/shard_map/prune/pallas_call | solution.py:329
  19.6 7.3 %all-to-all-start = ((f32[32,1,128]{2,1,0:T(1,128)}), f32[32,1,128]{2,1,0:T(1,128)S(1)}, u32[]{:S(2)}, u32[]{:S(2)}) async-start(f32[32,1,128]{2,1,0:T(1,128)} %get-tuple-element.6), calls=%async_computation | async-start | bytes 32768 | tf_op jit(solution)/shard_map/all_to_all | solution.py:360
  26.9 7.1 %all-to-all-done = f32[32,1,128]{2,1,0:T(1,128)S(1)} async-done(((f32[32,1,128]{2,1,0:T(1,128)}), f32[32,1,128]{2,1,0:T(1,128)S(1)}, u32[]{:S(2)}, u32[]{:S(2)}) %all-to-all-start) | async-done | bytes 16416 | tf_op jit(solution)/shard_map/all_to_all | solution.py:360
  34.0 0.6 %slice_reduce_fusion = f32[]{:T(128)} fusion(f32[4,8,128]{2,1,0:T(8,128)S(1)} %bitcast.9), kind=kLoop, calls=%fused_computation | loop fusion | flops 2047 | bytes 8196 | tf_op jit(solution)/shard_map/reduce_sum | solution.py:365
  34.7 0.6 %fusion = f32[1,64]{1,0:T(1,128)} fusion(f32[128]{0:T(128)S(1)} %dynamic-slice_reduce_fusion), kind=kLoop, calls=%fused_computation.3 | loop fusion | flops 64 | bytes 768 | tf_op jit(solution)/shard_map/broadcast_in_dim | solution.py:366
  (1 shorter events, 0.0 us)
Async XLA Ops:
  19.6 14.5 %all-to-all-start = ((f32[32,1,128]{2,1,0:T(1,128)}), f32[32,1,128]{2,1,0:T(1,128)S(1)}, u32[]{:S(2)}, u32[]{:S(2)}) async-start(f32[32,1,128]{2,1,0:T(1,128)} %get-tuple-element.6), calls=%async_computation | async-start | bytes 32768 | tf_op jit(solution)/shard_map/all_to_all | solution.py:360
